TPU v7x, 256 devices: a whole 4x4x8 slice. The times are simulated.
256 devices in a mesh: expert: 8 (over x, core), latent: 32 (over y, z).
Axes of the slice: x: 4, y: 4, z: 8, core: 2. Of those that a mesh axis runs over, the one named last changes fastest.
Arguments:
- tokens: bfloat16 [2048, 2560], P(('expert', 'latent')), may hold values from -6 to 6
- route: int32 [2048, 1], P(('expert', 'latent')), may hold values from 0 to 7; in each aligned block of 8 rows (0 to 7, 8 to 15, ...) at most 2 rows name the same one
- blocks: int32 [2048, 64], P(('expert', 'latent')), may hold values from 0 to 255, all different within a row
- weight: bfloat16 [8, 2560, 32768], P('expert', None, 'latent'), may hold values from -0.125 to 0.125
- enc_bias: float32 [8, 32768], P('expert', 'latent'), may hold values from -3 to 3
- dec_bias: float32 [2560], replicated, may hold values from -3 to 3
Outputs:
- grad_weight: bfloat16 [8, 2560, 32768], P('expert', None, 'latent')
- grad_enc: float32 [8, 32768], P('expert', 'latent')
- grad_dec: float32 [2560], replicated
- loss: float32 [], replicated
Inputs may be any that keep to these rules, and one draw needn't show every extreme that they name: `route`: within the rows of one device (aligned blocks of 8 rows) no expert is named by more than 2 rows. Each row lists 64 different blocks.
All inputs are finite; a program needn't handle non-finite values.
Results may differ from a plain program's by a relative error of at most 0.012.
The roundings to bfloat16 on the way count: a program that leaves them out, or rounds other values in their place, can miss the bound.
Values may be sent and summed in bfloat16 or wider, within the bound.
No kernel may reach another device: no remote copies, remote signals or barrier semaphores. Data moves between devices by JAX's collectives and lax.ppermute only.
A program may use at most 128 MiB of HBM per device.

v0:
```python
import jax
import jax.numpy as jnp
from jax import lax
from jax.sharding import PartitionSpec as P

BLK = 128
CAP = 2


def shards(tokens, route, blocks, weight, enc_bias, dec_bias):
    n_expert = lax.axis_size("expert")
    n_latent = lax.axis_size("latent")
    width = tokens.shape[1]
    list_len = blocks.shape[1]
    expert_of = route[:, 0]
    one_hot = (expert_of[:, None] == jnp.arange(n_expert, dtype=jnp.int32)[None, :]).astype(
        jnp.int32
    )
    earlier = jnp.sum((jnp.cumsum(one_hot, axis=0) - one_hot) * one_hot, axis=1)
    target = expert_of * CAP + earlier
    send_rows = jnp.zeros((n_expert * CAP, width), jnp.bfloat16).at[target].set(tokens)
    send_rows = send_rows.reshape(n_expert, CAP, width)
    send_lists = jnp.full((n_expert * CAP, list_len), -1, jnp.int32).at[target].set(blocks)
    send_lists = send_lists.reshape(n_expert, CAP, list_len)
    got_rows, got_lists = (
        lax.all_to_all(send_rows, "expert", split_axis=0, concat_axis=0, tiled=True),
        lax.all_to_all(send_lists, "expert", split_axis=0, concat_axis=0, tiled=True),
    )
    all_rows, all_lists = (
        lax.all_gather(got_rows[None], "latent", axis=0, tiled=True),
        lax.all_gather(got_lists[None], "latent", axis=0, tiled=True),
    )
    token_rows = all_rows.reshape(-1, width)
    listed = all_lists.reshape(-1, list_len)
    row_count = token_rows.shape[0]
    valid = (listed[:, 0] >= 0).astype(jnp.float32)
    slice_index = lax.axis_index("latent")
    weights_here = weight[0]
    per_slice = weights_here.shape[1] // BLK
    own_blocks = slice_index * per_slice + jnp.arange(per_slice, dtype=jnp.int32)
    chosen = jnp.any(listed[:, :, None] == own_blocks[None, None, :], axis=1).astype(jnp.float32)
    mask = jnp.repeat(chosen, BLK, axis=1)
    rows_f32 = token_rows.astype(jnp.float32)
    shifted = (rows_f32 - dec_bias).astype(jnp.bfloat16)
    pre_act = jnp.dot(shifted, weights_here, preferred_element_type=jnp.float32) + enc_bias[0]
    active = jnp.maximum(pre_act, 0.0) * mask
    active_bf = active.astype(jnp.bfloat16)
    share = row_count // n_latent
    first_row = slice_index * share
    along_width = (((1,), (1,)), ((), ()))
    partial_sum = lax.dot_general(
        active_bf, weights_here, along_width, preferred_element_type=jnp.float32
    )
    summed = lax.psum(partial_sum, "latent")
    error_all = (summed + dec_bias - rows_f32) * valid[:, None]
    error_bf = error_all.astype(jnp.bfloat16)
    error_share = lax.dynamic_slice_in_dim(error_all, first_row, share, 0)
    grad_act = jnp.dot(error_bf, weights_here, preferred_element_type=jnp.float32)
    grad_pre = grad_act * (pre_act > 0.0).astype(jnp.float32) * mask
    grad_pre_bf = grad_pre.astype(jnp.bfloat16)
    along_rows = (((0,), (0,)), ((), ()))
    grad_here = lax.dot_general(
        shifted, grad_pre_bf, along_rows, preferred_element_type=jnp.float32
    )
    grad_here = grad_here + lax.dot_general(
        error_bf, active_bf, along_rows, preferred_element_type=jnp.float32
    )
    grad_bias = jnp.sum(grad_pre, axis=0)
    pulled = jnp.dot(
        weights_here, grad_bias.astype(jnp.bfloat16), preferred_element_type=jnp.float32
    )
    bias_term = jnp.sum(error_share, axis=0) - pulled
    loss_term = 0.5 * jnp.sum(error_share * error_share)
    grad_dec, loss_sum = lax.psum((bias_term, loss_term), ("expert", "latent"))
    loss = loss_sum / (tokens.shape[0] * n_expert * n_latent)
    return (grad_here.astype(jnp.bfloat16)[None], grad_bias[None], grad_dec, loss)


def solution(mesh):
    return jax.shard_map(
        shards,
        mesh=mesh,
        in_specs=(
            P(("expert", "latent"), None),
            P(("expert", "latent"), None),
            P(("expert", "latent"), None),
            P("expert", None, "latent"),
            P("expert", "latent"),
            P(),
        ),
        out_specs=(P("expert", None, "latent"), P("expert", "latent"), P(), P()),
        check_vma=False,
    )
```

profile of v0, /device:TPU:1, one launch (start us, length us, event | category | flops | bytes accessed | tf_op | source)
XLA Modules:
  0.0 402.3 jit_solution(3232776257881222928)
XLA Ops:
  7.2 0.0 all-gather.4.cloned.1.call-start
  7.2 0.7 fusion.24
  8.0 0.8 select_reduce_fusion
  8.8 0.7 fusion.25
  9.5 0.9 scatter_custom_fusion
  10.4 11.2 %all_to_all.10 = bf16[8,2,2560]{2,1,0:T(2,128)(2,1)} all-to-all(bf16[8,2,2560]{2,1,0:T(2,128)(2,1)S(1)} %reshape.33), channel_id=1, replica_groups=mesh['expert'=8,'latent'=32] {'expert'}, dimensions={0} | all-to-all | bytes 163840 | tf_op jit(solution)/shard_map/all_to_all | solution.py:26
  21.6 0.0 all-gather.4.cloned.1.call-update
  21.7 0.8 scatter_custom_fusion.1
  22.4 0.7 reshape.68
  23.1 4.0 all-to-all-start.1
  27.1 4.5 %all-to-all-done.1 = s32[8,1,128]{2,1,0:T(1,128)S(1)} async-done(((s32[8,1,128]{2,1,0:T(1,128)}), s32[8,1,128]{2,1,0:T(1,128)S(1)}, u32[]{:S(2)}, u32[]{:S(2)}) %all-to-all-start.1) | async-done | bytes 4128 | tf_op jit(solution)/shard_map/all_to_all | solution.py:27
  31.6 0.5 broadcast.43
  32.2 0.7 reduce.4
  32.8 0.1 reshape.69
  32.9 40.8 %all-gather.1 = s32[256,2,64]{2,1,0:T(2,128)S(1)} all-gather(s32[8,2,64]{2,1,0:T(2,128)S(1)} %reshape.69), channel_id=3, replica_groups=mesh['expert'=8,'latent'=32] {'latent'}, dimensions={0}, use_global_device_ids=true | all-gather | bytes 135168 | tf_op jit(solution)/shard_map/all_gather | solution.py:31
  73.7 0.1 copy.12
  73.8 0.2 compare_reduce_fusion
  74.1 0.1 copy.13
  74.2 24.0 %all-gather.4.cloned.1.call-done = bf16[256,2,2560]{2,1,0:T(2,128)(2,1)} async-done(((bf16[8,2,2560]{2,1,0:T(2,128)(2,1)}), bf16[256,2,2560]{2,1,0:T(2,128)(2,1)}) %all-gather.4.cloned.1.call-update) | async-done | bytes 2621456 | tf_op jit(solution)/shard_map/all_gather | solution.py:30
  98.1 3.5 convert_element_type.56
  101.7 2.3 subtract_convert_fusion
  104.0 0.0 copy-start.6
  104.0 2.6 convert_element_type.47
  106.6 0.6 broadcast_in_dim.32
  107.2 0.0 copy-start.1
  107.2 0.0 copy-done.6
  107.2 0.0 slice-start.3
  107.3 8.7 %fusion.11 = (bf16[512,1024]{1,0:T(8,128)(2,1)S(1)}, f32[512,1024]{1,0:T(8,128)}) fusion(f32[64,8,8,128]{3,2,1,0:T(8,128)S(1)} %bitcast.51, f32[1024]{0:T(1024)S(1)} %bitcast.57, bf16[512,2560]{1,0:T(8,128)(2,1)} %convert_element_type.47, bf16[1,2560,1024]{2,1,0:T(8,128)(2,1)} %param.9), kind=kOutput, calls=%fused_computation.19 | convolution fusion | flops 2686451712 | bytes 13111296 | tf_op jit(solution)/shard_map/dot_general | solution.py:45
  116.0 1.0 copy-done.3
  117.0 4.7 %fusion.4 = f32[512,2560]{1,0:T(8,128)} fusion(bf16[512,1024]{1,0:T(8,128)(2,1)S(1)} %get-tuple-element.8, bf16[1,2560,1024]{2,1,0:T(8,128)(2,1)S(1)} %bitcast.46), kind=kOutput, calls=%fused_computation.7 | convolution fusion | flops 2684354560 | bytes 11534336 | tf_op jit(solution)/shard_map/dot_general | solution.py:51
  121.7 0.0 all-reduce.3.cloned.1.call-update
  121.7 0.1 convert_reduce_fusion
  121.8 1.6 copy-done
  123.4 2.9 reshape.36
  126.4 168.2 %all-reduce.3.cloned.1.call-done = f32[512,2560]{1,0:T(8,128)} async-done(((f32[512,2560]{1,0:T(8,128)}), f32[512,2560]{1,0:T(8,128)}) %all-reduce.3.cloned.1.call-update) | async-done | bytes 5242896 | tf_op jit(solution)/shard_map/psum | solution.py:54
  294.5 4.9 %subtract_multiply_fusion = f32[512,2560]{1,0:T(8,128)S(1)} fusion(f32[512,2560]{1,0:T(8,128)} %reshape.36, f32[512,2560]{1,0:T(8,128)} %all-reduce.3.cloned.1.call-done, f32[512]{0:T(512)S(1)} %convert_reduce_fusion, f32[2560]{0:T(1024)S(1)} %copy-done.4), kind=kLoop, calls=%fused_computation.11 | loop fusion | flops 3932160 | bytes 15740928 | tf_op jit(solution)/shard_map/mul | solution.py:55
  299.5 0.0 slice-start.1
  299.5 5.9 %fusion.26 = (f32[1024]{0:T(1024)S(1)}, bf16[512,1024]{1,0:T(8,128)(2,1)S(1)}) fusion(f32[64,8,8,128]{3,2,1,0:T(8,128)S(1)} %bitcast.52, bf16[1,2560,1024]{2,1,0:T(8,128)(2,1)} %param.9, f32[512,2560]{1,0:T(8,128)S(1)} %subtract_multiply_fusion, f32[512,1024]{1,0:T(8,128)S(1)} %copy-done.7, f32[1024]{0:T(1024)S(1)} %bitcast.58), kind=kOutput, calls=%fused_computation.40 | convolution fusion | flops 2688809984 | bytes 15736832 | tf_op jit(solution)/shard_map/dot_general | solution.py:58
  305.4 0.0 copy-start.5
  305.4 0.0 slice-done
  305.4 0.0 slice-done.1
  305.4 0.0 slice-start.4
  305.5 3.0 fusion.9
  308.5 0.0 slice-start.5
  308.5 6.5 %fusion.8 = bf16[1,2560,1024]{2,1,0:T(8,128)(2,1)} fusion(f32[2560,1024]{1,0:T(8,128)S(1)} %fusion.9, bf16[512,1024]{1,0:T(8,128)(2,1)} %copy-done.3, f32[512,2560]{1,0:T(8,128)S(1)} %subtract_multiply_fusion), kind=kOutput, calls=%fused_computation.14 | convolution fusion | flops 2690908160 | bytes 22020096 | tf_op jit(solution)/shard_map/dot_general | solution.py:65
  315.0 0.6 multiply_reduce_fusion
  315.6 1.5 fusion.16
  317.8 75.9 %all-reduce = (f32[2560]{0:T(1024)}, f32[]{:T(128)}) all-reduce(f32[2560]{0:T(1024)S(1)} %sub.28, f32[]{:T(128)S(6)} %mul_shard_map.3), channel_id=1, replica_groups=mesh['expert'=8,'latent'=32] {'expert','latent'}, use_global_device_ids=true, to_apply=%region_8.9 | all-reduce | flops 2561 | bytes 20488 | tf_op jit(solution)/shard_map/psum | solution.py:74
  (27 shorter events, 0.1 us)
Async XLA Ops:
  7.2 94.5 %copy-start.4 = (f32[2560]{0:T(1024)S(1)}, f32[2560]{0:T(1024)}, u32[]{:S(2)}) copy-start(f32[2560]{0:T(1024)} %param.11) | copy-start | bytes 30724
  7.2 91.0 %all-gather.4.cloned.1.call-start = ((), (), s32[]{:S(2)}) async-start(), calls=%async_computation.3 | async-start | bytes 2703360 | tf_op jit(solution)/shard_map/all_gather | solution.py:30
  23.1 8.5 %all-to-all-start.1 = ((s32[8,1,128]{2,1,0:T(1,128)}), s32[8,1,128]{2,1,0:T(1,128)S(1)}, u32[]{:S(2)}, u32[]{:S(2)}) async-start(s32[8,1,128]{2,1,0:T(1,128)} %reshape.68), calls=%async_computation.1 | async-start | bytes 8192 | tf_op jit(solution)/shard_map/all_to_all | solution.py:27
  27.1 267.4 %all-reduce.3.cloned.1.call-start = ((), (), s32[]{:S(2)}) async-start(), calls=%async_computation.2 | async-start | bytes 10485760 | tf_op jit(solution)/shard_map/psum | solution.py:54
  104.0 3.2 copy-start.6
  106.6 10.4 %slice-start.2 = ((s8[5242880]{0:T(1024)(128)(4,1)}), s8[4194304]{0:T(1024)(128)(4,1)S(1)}, s32[]{:S(2)}) async-start(s8[5242880]{0:T(1024)(128)(4,1)} %bitcast.45), calls=%async_computation.6 | async-start | bytes 8388608
  107.2 8.8 %copy-start.1 = (f32[512,8,128]{2,1,0:T(8,128)}, f32[512,8,128]{2,1,0:T(8,128)S(1)}, u32[]{:S(2)}) copy-start(f32[512,8,128]{2,1,0:T(8,128)S(1)} %broadcast_in_dim.32) | copy-start | bytes 6291460
  107.2 9.7 %slice-start.3 = ((s8[5242880]{0:T(1024)(128)(4,1)}), s8[1048576]{0:T(1024)(128)(4,1)S(1)}, s32[]{:S(2)}) async-start(s8[5242880]{0:T(1024)(128)(4,1)} %bitcast.45), calls=%async_computation.7 | async-start | bytes 2097152
  116.0 1.0 copy-start.3
  121.7 1.7 copy-start
  126.3 173.1 %copy-start.2 = (f32[512,8,128]{2,1,0:T(8,128)S(1)}, f32[512,8,128]{2,1,0:T(8,128)}, u32[]{:S(2)}) copy-start(f32[512,8,128]{2,1,0:T(8,128)} %copy-done.1) | copy-start | bytes 6291460
  294.5 4.9 %copy-start.7 = (f32[512,1024]{1,0:T(8,128)S(1)}, f32[512,1024]{1,0:T(8,128)}, u32[]{:S(2)}) copy-start(f32[512,1024]{1,0:T(8,128)} %get-tuple-element.9) | copy-start | bytes 6291460
  294.5 10.9 %slice-start = ((s8[5242880]{0:T(1024)(128)(4,1)}), s8[1048576]{0:T(1024)(128)(4,1)S(1)}, s32[]{:S(2)}) async-start(s8[5242880]{0:T(1024)(128)(4,1)} %bitcast.42), calls=%async_computation.4 | async-start | bytes 2097152
  299.5 6.0 %slice-start.1 = ((s8[5242880]{0:T(1024)(128)(4,1)}), s8[4194304]{0:T(1024)(128)(4,1)S(1)}, s32[]{:S(2)}) async-start(s8[5242880]{0:T(1024)(128)(4,1)} %bitcast.42), calls=%async_computation.5 | async-start | bytes 8388608
  305.4 10.2 %copy-start.5 = (f32[1024]{0:T(1024)}, f32[1024]{0:T(1024)S(1)}, u32[]{:S(2)}) copy-start(f32[1024]{0:T(1024)S(1)} %get-tuple-element.10) | copy-start | bytes 12292
  305.4 10.2 %slice-start.4 = ((s8[5242880]{0:T(1024)(128)(4,1)}), s8[4194304]{0:T(1024)(128)(4,1)S(1)}, s32[]{:S(2)}) async-start(s8[5242880]{0:T(1024)(128)(4,1)} %bitcast.47), calls=%async_computation.8 | async-start | bytes 8388608
  308.5 7.2 %slice-start.5 = ((s8[5242880]{0:T(1024)(128)(4,1)}), s8[1048576]{0:T(1024)(128)(4,1)S(1)}, s32[]{:S(2)}) async-start(s8[5242880]{0:T(1024)(128)(4,1)} %bitcast.47), calls=%async_computation.9 | async-start | bytes 2097152
Sparse Core Ops, SparseCore 0:
  21.8 76.3 all-gather.3
  121.8 172.6 all-reduce.2
where the time goes:
time: 403 us; the launch traced here: 402 us
  waiting for transfers between devices  197 us (49%)
  blocking collectives  128 us (32%)
  matrix products  30.3 us (8%)
  between operations  16.7 us (4%)
  other arithmetic  14.6 us (4%)
  local copies, waits for them, and re-layouts  12 us (3%)
  starting transfers between devices  4.05 us (1%)
    psum x1, waiting for transfers between devices, shards(): summed = lax.psum(partial_sum, 'latent')  168 us
    psum x1, blocking collectives, shards(): grad_dec, loss_sum = lax.psum((bias_term, loss_term), ('expert', 'latent'))  75.9 us
    all_gather x1, blocking collectives, shards(): lax.all_gather(got_lists[None], 'latent', axis=0, tiled=True)  40.8 us
    all_gather x1, waiting for transfers between devices, shards(): lax.all_gather(got_rows[None], 'latent', axis=0, tiled=True)  24 us
    all_to_all x1, blocking collectives, shards(): lax.all_to_all(send_rows, 'expert', split_axis=0, concat_axis=0, tiled=True)  11.2 us
    dot_general x1, matrix products, shards(): jnp.dot(shifted, weights_here, preferred_element_type=jnp.float32)  8.73 us
  transfers between devices with their start and end apart: 3, of which 3 were waited for; matrix products, arithmetic and copies ran while one was open for 2% of the time, Pallas kernels for 0%

commit v1 on v0

--- a/solution.py
+++ b/solution.py
@@ -27,7 +27,10 @@
         lax.all_to_all(send_lists, "expert", split_axis=0, concat_axis=0, tiled=True),
     )
     all_rows, all_lists = (
-        lax.all_gather(got_rows[None], "latent", axis=0, tiled=True),
+        jnp.concatenate(
+            lax.all_to_all(jnp.stack([got_rows[None]] * lax.axis_size("latent")), "latent", 0, 0),
+            axis=0,
+        ),
         lax.all_gather(got_lists[None], "latent", axis=0, tiled=True),
     )
     token_rows = all_rows.reshape(-1, width)

time: 403 us -> 449 us (1.11)
  blocking collectives: 128 us -> 172 us
  waiting for transfers between devices: 197 us -> 181 us
  starting transfers between devices: 4.05 us -> 17 us
  local copies, waits for them, and re-layouts: 12 us -> 18.3 us
    all_gather x1, blocking collectives: 40.8 us -> 88.5 us  [shards(): lax.all_gather(got_lists[None], 'latent', axis=0, tiled=True)]
    all_gather x1 -> x0, waiting for transfers between devices: 24 us -> none  [shards(): lax.all_gather(got_rows[None], 'latent', axis=0, tiled=True)]
    all_to_all x0 -> x1, starting transfers between devices: none -> 10.5 us  [shards(): lax.all_to_all(jnp.stack([got_rows[None]] * lax.axis_size('latent')), 'la...]
    psum x1, waiting for transfers between devices: 168 us -> 177 us  [shards(): summed = lax.psum(partial_sum, 'latent')]
  transfers between devices with their start and end apart: 3 -> 3, of which waited for: 3 -> 2; matrix products, arithmetic and copies ran while one was open for 2% -> 1% of each run, Pallas kernels for 0% -> 0%
where the time goes in v1:
time: 449 us
  waiting for transfers between devices  181 us (40%)
  blocking collectives  172 us (38%)
  matrix products  30.3 us (7%)
  local copies, waits for them, and re-layouts  18.3 us (4%)
  starting transfers between devices  17 us (4%)
  between operations  16.7 us (4%)
  other arithmetic  13.1 us (3%)
    psum x1, waiting for transfers between devices, shards(): summed = lax.psum(partial_sum, 'latent')  177 us
    all_gather x1, blocking collectives, shards(): lax.all_gather(got_lists[None], 'latent', axis=0, tiled=True)  88.5 us
    psum x1, blocking collectives, shards(): grad_dec, loss_sum = lax.psum((bias_term, loss_term), ('expert', 'latent'))  75.9 us
    all_to_all x1, starting transfers between devices, shards(): lax.all_to_all(jnp.stack([got_rows[None]] * lax.axis_size('latent')), 'la...  10.5 us
  transfers between devices with their start and end apart: 3, of which 2 were waited for; matrix products, arithmetic and copies ran while one was open for 1% of the time, Pallas kernels for 0%

profile of v1, /device:TPU:1, one launch (start us, length us, event | category | flops | bytes accessed | tf_op | source)
XLA Modules:
  0.0 448.6 jit_solution(16160862069241635782)
XLA Ops:
  7.2 0.0 copy-start.3
  7.2 0.7 fusion.24
  7.9 0.8 select_reduce_fusion
  8.8 0.7 fusion.25
  9.4 0.8 scatter_custom_fusion.1
  10.2 0.7 reshape.65
  10.9 6.5 %all-to-all-start.2 = ((s32[8,1,128]{2,1,0:T(1,128)}), s32[8,1,128]{2,1,0:T(1,128)S(1)}, u32[]{:S(2)}, u32[]{:S(2)}) async-start(s32[8,1,128]{2,1,0:T(1,128)} %reshape.65), calls=%async_computation.2 | async-start | bytes 8192 | tf_op jit(solution)/shard_map/all_to_all | solution.py:27
  17.3 0.9 scatter_custom_fusion
  18.3 3.6 all-to-all-done.2
  21.8 8.0 %all_to_all.15 = bf16[8,2,2560]{2,1,0:T(2,128)(2,1)S(1)} all-to-all(bf16[8,2,2560]{2,1,0:T(2,128)(2,1)S(1)} %reshape.34), channel_id=1, replica_groups=mesh['expert'=8,'latent'=32] {'expert'}, dimensions={0} | all-to-all | bytes 163840 | tf_op jit(solution)/shard_map/all_to_all | solution.py:26
  29.8 3.9 stack.3
  33.7 10.5 %all-to-all-start.1 = ((bf16[32,1,8,2,2560]{4,3,2,1,0:T(2,128)(2,1)}), bf16[32,1,8,2,2560]{4,3,2,1,0:T(2,128)(2,1)S(1)}, u32[]{:S(2)}, u32[]{:S(2)}) async-start(bf16[32,1,8,2,2560]{4,3,2,1,0:T(2,128)(2,1)} %stack.3), calls=%async_computation.1 | async-start | bytes 5242880 | tf_op jit(solution)/shard_map/all_to_all | solution.py:31
  44.2 0.0 all-reduce.3.cloned.1.call-start
  44.3 0.5 broadcast.45
  44.8 0.7 reduce.4
  45.5 0.1 reshape.66
  45.5 88.5 %all-gather = s32[256,2,64]{2,1,0:T(2,128)S(1)} all-gather(s32[8,2,64]{2,1,0:T(2,128)S(1)} %reshape.66), channel_id=2, replica_groups=mesh['expert'=8,'latent'=32] {'latent'}, dimensions={0}, use_global_device_ids=true | all-gather | bytes 135168 | tf_op jit(solution)/shard_map/all_gather | solution.py:34
  134.0 0.1 copy.12
  134.1 0.2 compare_reduce_fusion
  134.4 0.1 copy.13
  134.5 0.0 copy-start.5
  134.5 0.0 all-to-all-done.1
  134.5 0.0 copy-done.3
  134.5 4.3 subtract_convert_fusion
  138.8 6.7 %convert_element_type.47 = bf16[512,2560]{1,0:T(8,128)(2,1)} reshape(bf16[32,1,8,2,2560]{4,3,2,1,0:T(2,128)(2,1)} %subtract_convert_fusion) | data formatting | bytes 5242880 | tf_op jit(solution)/shard_map/convert_element_type | solution.py:47
  145.5 0.6 broadcast_in_dim.28
  146.1 0.0 copy-start
  146.1 0.0 copy-done.5
  146.1 0.0 slice-start.3
  146.1 8.8 %fusion.11 = (bf16[512,1024]{1,0:T(8,128)(2,1)S(1)}, f32[512,1024]{1,0:T(8,128)}) fusion(f32[64,8,8,128]{3,2,1,0:T(8,128)S(1)} %bitcast.49, f32[1024]{0:T(1024)S(1)} %bitcast.55, bf16[512,2560]{1,0:T(8,128)(2,1)} %convert_element_type.47, bf16[1,2560,1024]{2,1,0:T(8,128)(2,1)} %param.9), kind=kOutput, calls=%fused_computation.19 | convolution fusion | flops 2686451712 | bytes 13111296 | tf_op jit(solution)/shard_map/dot_general | solution.py:48
  154.9 0.0 copy-done
  154.9 1.0 copy-done.2
  155.9 4.7 %fusion.4 = f32[512,2560]{1,0:T(8,128)} fusion(bf16[512,1024]{1,0:T(8,128)(2,1)S(1)} %get-tuple-element.8, bf16[1,2560,1024]{2,1,0:T(8,128)(2,1)S(1)} %bitcast.44), kind=kOutput, calls=%fused_computation.7 | convolution fusion | flops 2684354560 | bytes 11534336 | tf_op jit(solution)/shard_map/dot_general | solution.py:54
  160.6 0.0 all-reduce.3.cloned.1.call-update
  160.6 0.1 convert_reduce_fusion
  160.8 2.9 reshape.37
  163.7 177.3 %all-reduce.3.cloned.1.call-done = f32[512,2560]{1,0:T(8,128)} async-done(((f32[512,2560]{1,0:T(8,128)}), f32[512,2560]{1,0:T(8,128)}) %all-reduce.3.cloned.1.call-update) | async-done | bytes 5242896 | tf_op jit(solution)/shard_map/psum | solution.py:57
  341.0 4.9 %subtract_multiply_fusion = f32[512,2560]{1,0:T(8,128)S(1)} fusion(f32[512,2560]{1,0:T(8,128)} %reshape.37, f32[512,2560]{1,0:T(8,128)} %all-reduce.3.cloned.1.call-done, f32[512]{0:T(512)S(1)} %convert_reduce_fusion, f32[2560]{0:T(1024)S(1)} %copy-done.3), kind=kLoop, calls=%fused_computation.11 | loop fusion | flops 3932160 | bytes 15740928 | tf_op jit(solution)/shard_map/mul | solution.py:58
  345.9 0.0 slice-start.1
  345.9 5.9 %fusion.26 = (f32[1024]{0:T(1024)S(1)}, bf16[512,1024]{1,0:T(8,128)(2,1)S(1)}) fusion(f32[64,8,8,128]{3,2,1,0:T(8,128)S(1)} %bitcast.50, bf16[1,2560,1024]{2,1,0:T(8,128)(2,1)} %param.9, f32[512,2560]{1,0:T(8,128)S(1)} %subtract_multiply_fusion, f32[512,1024]{1,0:T(8,128)S(1)} %copy-done.6, f32[1024]{0:T(1024)S(1)} %bitcast.56), kind=kOutput, calls=%fused_computation.40 | convolution fusion | flops 2688809984 | bytes 15736832 | tf_op jit(solution)/shard_map/dot_general | solution.py:61
  351.8 0.0 copy-start.4
  351.8 0.0 slice-start.4
  351.8 3.0 fusion.9
  354.8 0.0 slice-start.5
  354.8 6.5 %fusion.8 = bf16[1,2560,1024]{2,1,0:T(8,128)(2,1)} fusion(f32[2560,1024]{1,0:T(8,128)S(1)} %fusion.9, bf16[512,1024]{1,0:T(8,128)(2,1)} %copy-done.2, f32[512,2560]{1,0:T(8,128)S(1)} %subtract_multiply_fusion), kind=kOutput, calls=%fused_computation.14 | convolution fusion | flops 2690908160 | bytes 22020096 | tf_op jit(solution)/shard_map/dot_general | solution.py:68
  361.3 0.6 multiply_reduce_fusion
  362.0 1.5 fusion.16
  364.1 75.9 %all-reduce = (f32[2560]{0:T(1024)}, f32[]{:T(128)}) all-reduce(f32[2560]{0:T(1024)S(1)} %sub.28, f32[]{:T(128)S(6)} %mul_shard_map.3), channel_id=1, replica_groups=mesh['expert'=8,'latent'=32] {'expert','latent'}, use_global_device_ids=true, to_apply=%region_8.9 | all-reduce | flops 2561 | bytes 20488 | tf_op jit(solution)/shard_map/psum | solution.py:77
  (24 shorter events, 0.1 us)
Async XLA Ops:
  7.2 127.3 %copy-start.3 = (f32[2560]{0:T(1024)S(1)}, f32[2560]{0:T(1024)}, u32[]{:S(2)}) copy-start(f32[2560]{0:T(1024)} %param.11) | copy-start | bytes 30724
  10.9 11.0 %all-to-all-start.2 = ((s32[8,1,128]{2,1,0:T(1,128)}), s32[8,1,128]{2,1,0:T(1,128)S(1)}, u32[]{:S(2)}, u32[]{:S(2)}) async-start(s32[8,1,128]{2,1,0:T(1,128)} %reshape.65), calls=%async_computation.2 | async-start | bytes 8192 | tf_op jit(solution)/shard_map/all_to_all | solution.py:27
  33.7 100.8 %all-to-all-start.1 = ((bf16[32,1,8,2,2560]{4,3,2,1,0:T(2,128)(2,1)}), bf16[32,1,8,2,2560]{4,3,2,1,0:T(2,128)(2,1)S(1)}, u32[]{:S(2)}, u32[]{:S(2)}) async-start(bf16[32,1,8,2,2560]{4,3,2,1,0:T(2,128)(2,1)} %stack.3), calls=%async_computation.1 | async-start | bytes 5242880 | tf_op jit(solution)/shard_map/all_to_all | solution.py:31
  44.2 296.8 %all-reduce.3.cloned.1.call-start = ((), (), s32[]{:S(2)}) async-start(), calls=%async_computation.3 | async-start | bytes 10485760 | tf_op jit(solution)/shard_map/psum | solution.py:57
  134.5 11.6 %copy-start.5 = (f32[1,1024]{1,0:T(1,128)S(1)}, f32[1,1024]{1,0:T(1,128)}, u32[]{:S(2)}) copy-start(f32[1,1024]{1,0:T(1,128)} %param.10) | copy-start | bytes 12292
  145.5 10.4 %slice-start.2 = ((s8[5242880]{0:T(1024)(128)(4,1)}), s8[4194304]{0:T(1024)(128)(4,1)S(1)}, s32[]{:S(2)}) async-start(s8[5242880]{0:T(1024)(128)(4,1)} %bitcast.43), calls=%async_computation.6 | async-start | bytes 8388608
  146.1 8.8 %copy-start = (f32[512,8,128]{2,1,0:T(8,128)}, f32[512,8,128]{2,1,0:T(8,128)S(1)}, u32[]{:S(2)}) copy-start(f32[512,8,128]{2,1,0:T(8,128)S(1)} %broadcast_in_dim.28) | copy-start | bytes 6291460
  146.1 9.8 %slice-start.3 = ((s8[5242880]{0:T(1024)(128)(4,1)}), s8[1048576]{0:T(1024)(128)(4,1)S(1)}, s32[]{:S(2)}) async-start(s8[5242880]{0:T(1024)(128)(4,1)} %bitcast.43), calls=%async_computation.7 | async-start | bytes 2097152
  154.9 1.0 copy-start.2
  163.7 182.1 %copy-start.1 = (f32[512,8,128]{2,1,0:T(8,128)S(1)}, f32[512,8,128]{2,1,0:T(8,128)}, u32[]{:S(2)}) copy-start(f32[512,8,128]{2,1,0:T(8,128)} %copy-done) | copy-start | bytes 6291460
  341.0 4.9 %copy-start.6 = (f32[512,1024]{1,0:T(8,128)S(1)}, f32[512,1024]{1,0:T(8,128)}, u32[]{:S(2)}) copy-start(f32[512,1024]{1,0:T(8,128)} %get-tuple-element.9) | copy-start | bytes 6291460
  341.0 10.8 %slice-start = ((s8[5242880]{0:T(1024)(128)(4,1)}), s8[1048576]{0:T(1024)(128)(4,1)S(1)}, s32[]{:S(2)}) async-start(s8[5242880]{0:T(1024)(128)(4,1)} %bitcast.41), calls=%async_computation.4 | async-start | bytes 2097152
  345.9 6.0 %slice-start.1 = ((s8[5242880]{0:T(1024)(128)(4,1)}), s8[4194304]{0:T(1024)(128)(4,1)S(1)}, s32[]{:S(2)}) async-start(s8[5242880]{0:T(1024)(128)(4,1)} %bitcast.41), calls=%async_computation.5 | async-start | bytes 8388608
  351.8 10.2 %copy-start.4 = (f32[1024]{0:T(1024)}, f32[1024]{0:T(1024)S(1)}, u32[]{:S(2)}) copy-start(f32[1024]{0:T(1024)S(1)} %get-tuple-element.10) | copy-start | bytes 12292
  351.8 10.2 %slice-start.4 = ((s8[5242880]{0:T(1024)(128)(4,1)}), s8[4194304]{0:T(1024)(128)(4,1)S(1)}, s32[]{:S(2)}) async-start(s8[5242880]{0:T(1024)(128)(4,1)} %bitcast.45), calls=%async_computation.8 | async-start | bytes 8388608
  354.8 7.2 %slice-start.5 = ((s8[5242880]{0:T(1024)(128)(4,1)}), s8[1048576]{0:T(1024)(128)(4,1)S(1)}, s32[]{:S(2)}) async-start(s8[5242880]{0:T(1024)(128)(4,1)} %bitcast.45), calls=%async_computation.9 | async-start | bytes 2097152
Sparse Core Ops, SparseCore 0:
  160.8 180.1 all-reduce.2
